TPU v7x, 512 devices: a whole 4x4x16 slice. The times are simulated.
512 devices in a mesh: gz: 16 (over y, x), pa: 32 (over z, core).
Axes of the slice: x: 4, y: 4, z: 16, core: 2. Of those that a mesh axis runs over, the one named last changes fastest.
Arguments:
- particles: float32 [6, 1048576], P(None, ('gz', 'pa')), may hold values from -6 to 6
- slice_index: int32 [1048576], P(('gz', 'pa')), may hold values from 0 to 127
- moving: int32 [16, 32, 2], P('gz', 'pa'), may hold values from 0 to 384, as said below
- decay_rate: float32 [8], replicated, may hold values from 0.3 to 600
- wake_freq: float32 [8], replicated, may hold values from -3.140625 to 3.140625
- wake_amp: float32 [4, 8], replicated, may hold values from -3 to 3
Outputs:
- wake_kick: float32 [3, 2048], P(None, 'gz')
- particles_out: float32 [6, 1441792], P(None, ('gz', 'pa'))
Inputs may be any that keep to these rules, and one draw needn't show every extreme that they name: `moving`: each entry is at most 384, and some entry equals 384.
All inputs are finite; a program needn't handle non-finite values.
Results may differ from a plain program's by a relative error of at most 0.0003.
Values sent between devices are 32-bit elements; how exact they have to be, the bound alone decides.
No kernel may reach another device: no remote copies, remote signals or barrier semaphores. Data moves between devices by JAX's collectives and lax.ppermute only.
A program may use at most 64 MiB of HBM per device.

v0:
```python
import math
import jax
import jax.numpy as jnp
from jax import lax
from jax.sharding import PartitionSpec as P

S_DEV = 128
two_pi = 6.283185307179586
adjust_horiz = 0.269
adjust_vert = 0.355
chroma_horiz = 0.05
chroma_vert = 0.04
curve_horiz = 0.02
curve_vert = -0.015
detune_self = 0.03
detune_cross = -0.02
voltage = 0.05
synch_phase = 0.3
slippage = 0.1


def from_behind_2(value, axis, steps):
    count = lax.axis_size(axis)
    leading, last = (max(0, -steps), min(count, count - steps))
    return lax.ppermute(value, axis, [(source, source + steps) for source in range(leading, last)])


def complex_mul(first, second):
    return jnp.stack(
        [first[0] * second[0] - first[1] * second[1], first[0] * second[1] + first[1] * second[0]]
    )


def powers(damping, wake_freq, distance):
    envelope = jnp.exp(-damping[:, None] * distance[None, :])
    angles = wake_freq[:, None] * distance[None, :]
    return (envelope * jnp.cos(angles), envelope * jnp.sin(angles))


def toeplitz(wave):
    slab_width = wave.shape[0]
    row_index = lax.broadcasted_iota(jnp.int32, (slab_width, slab_width), 0)
    col_index = lax.broadcasted_iota(jnp.int32, (slab_width, slab_width), 1)
    offset = col_index - row_index
    picked = jnp.take(wave, jnp.clip(offset, 0, slab_width - 1))
    return jnp.where(offset > 0, picked, jnp.float32(0.0))


def slab_tables(decay_rate, wake_freq, wake_amp, slab_width, slice_total):
    damping = decay_rate / slice_total
    norm_trans = jnp.sqrt(2.0 * damping)
    norm_long = jnp.sqrt(damping * damping + wake_freq * wake_freq)
    coef_real = jnp.stack(
        [wake_amp[0] * norm_trans, wake_amp[0] * norm_trans, wake_amp[2] * norm_long], axis=1
    )
    coef_imag = jnp.stack(
        [wake_amp[1] * norm_trans, wake_amp[1] * norm_trans, wake_amp[3] * norm_long], axis=1
    )
    distance = jnp.arange(slab_width, dtype=jnp.float32)
    near_re, near_im = powers(damping, wake_freq, distance)
    far_re, far_im = powers(damping, wake_freq, slab_width - distance)
    whole_re, whole_im = powers(damping, wake_freq, jnp.full((1,), slab_width, jnp.float32))
    factor = jnp.stack(
        [jnp.broadcast_to(whole_re, coef_real.shape), jnp.broadcast_to(whole_im, coef_real.shape)]
    )
    wave_trans = jnp.sum(
        norm_trans[:, None] * (wake_amp[0][:, None] * near_re - wake_amp[1][:, None] * near_im),
        axis=0,
    )
    wave_long = jnp.sum(
        norm_long[:, None] * (wake_amp[2][:, None] * near_re - wake_amp[3][:, None] * near_im),
        axis=0,
    )
    return (
        toeplitz(wave_trans),
        toeplitz(wave_long),
        near_re,
        near_im,
        far_re,
        far_im,
        factor,
        coef_real,
        coef_imag,
    )


def slab_summary(moments, tables):
    highest = lax.Precision.HIGHEST
    return jnp.stack(
        [
            jnp.dot(tables[4], moments.T, precision=highest),
            jnp.dot(tables[5], moments.T, precision=highest),
        ]
    )


def slab_kick(moments, carried, tables):
    highest = lax.Precision.HIGHEST
    trans_kick = jnp.dot(moments[0:2], tables[0], precision=highest)
    long_kick = jnp.dot(moments[2:3], tables[1], precision=highest)
    coef_re = tables[7] * carried[0] - tables[8] * carried[1]
    coef_im = tables[7] * carried[1] + tables[8] * carried[0]
    incoming = jnp.dot(coef_re.T, tables[2], precision=highest) - jnp.dot(
        coef_im.T, tables[3], precision=highest
    )
    return jnp.concatenate([trans_kick, long_kick], axis=0) + incoming


def moment_values(particles, mean_fill):
    root_fill = math.sqrt(mean_fill)
    return jnp.stack(
        [
            particles[0] / root_fill,
            particles[2] / root_fill,
            jnp.full_like(particles[0], 1.0 / mean_fill),
        ]
    )


def deposit(values, index, segments):
    return jax.vmap(lambda column: jax.ops.segment_sum(column, index, num_segments=segments))(
        values
    )


def one_turn(coords, kicks):
    hor_pos = coords[0]
    hor_mom = coords[1] + kicks[0]
    ver_pos = coords[2]
    ver_mom = coords[3] + kicks[1]
    lag_pos = coords[4]
    energy_dev = coords[5] + kicks[2]
    action_x = 0.5 * (hor_pos * hor_pos + hor_mom * hor_mom)
    action_y = 0.5 * (ver_pos * ver_pos + ver_mom * ver_mom)
    phase_x = two_pi * (
        adjust_horiz
        + chroma_horiz * energy_dev
        + curve_horiz * energy_dev * energy_dev
        + detune_self * action_x
        + detune_cross * action_y
    )
    phase_y = two_pi * (
        adjust_vert
        + chroma_vert * energy_dev
        + curve_vert * energy_dev * energy_dev
        + detune_self * action_y
        + detune_cross * action_x
    )
    cosine_x = jnp.cos(phase_x)
    sine_x = jnp.sin(phase_x)
    cosine_y = jnp.cos(phase_y)
    sine_y = jnp.sin(phase_y)
    new_energy = energy_dev - voltage * (jnp.sin(synch_phase + lag_pos) - math.sin(synch_phase))
    new_lag = lag_pos - slippage * new_energy
    return jnp.stack(
        [
            cosine_x * hor_pos + sine_x * hor_mom,
            cosine_x * hor_mom - sine_x * hor_pos,
            cosine_y * ver_pos + sine_y * ver_mom,
            cosine_y * ver_mom - sine_y * ver_pos,
            new_lag,
            new_energy,
        ]
    )


def upstream(own_summary, factor, slab_count):

    def advance(step_index, carried):
        return from_behind_2(complex_mul(factor, carried) + own_summary, "gz", 1)

    return lax.fori_loop(0, slab_count - 1, advance, jnp.zeros_like(own_summary))


def body(particles, slice_index, moving, decay_rate, wake_freq, wake_amp):
    slab_count = lax.axis_size("gz")
    member_count = lax.axis_size("pa")
    local_count = particles.shape[1]
    slab_width = S_DEV
    tables = slab_tables(decay_rate, wake_freq, wake_amp, slab_width, slab_width * slab_count)
    mean_fill = local_count * member_count / slab_width
    values = moment_values(particles, mean_fill)
    partial_moments = deposit(values, slice_index, slab_width)
    moments = lax.psum(partial_moments, "pa")
    carried = upstream(slab_summary(moments, tables), tables[6], slab_count)
    wake_kick = slab_kick(moments, carried, tables)
    per_particle = jnp.take(wake_kick, slice_index, axis=1)
    capacity = local_count * 3 // 16
    head_count = moving[0, 0, 0]
    tail_count = moving[0, 0, 1]
    slot_index = lax.broadcasted_iota(jnp.int32, (1, capacity), 1)
    leaving_head = slot_index < head_count
    leaving_tail = slot_index >= capacity - tail_count
    zero_value = jnp.float32(0.0)
    tail_start = local_count - capacity
    moved_all = one_turn(particles, per_particle)
    head_part = moved_all[:, :capacity]
    tail_part = moved_all[:, tail_start:]
    head_send = jnp.where(leaving_head, head_part, zero_value)
    tail_send = jnp.where(leaving_tail, tail_part, zero_value)
    from_behind = from_behind_2(head_send, "gz", -1)
    from_ahead = from_behind_2(tail_send, "gz", 1)
    head_kept = jnp.where(leaving_head, zero_value, head_part)
    tail_kept = jnp.where(leaving_tail, zero_value, tail_part)
    middle_part = moved_all[:, capacity:tail_start]
    particles_out = jnp.concatenate(
        [from_behind, head_kept, middle_part, tail_kept, from_ahead], axis=1
    )
    return (wake_kick, particles_out)


def solution(mesh):
    return jax.shard_map(
        body,
        mesh=mesh,
        in_specs=(P(None, ("gz", "pa")), P(("gz", "pa")), P("gz", "pa", None), P(), P(), P()),
        out_specs=(P(None, "gz"), P(None, ("gz", "pa"))),
        check_vma=False,
    )
```

profile of v0, /device:TPU:16, one launch (start us, length us, event | category | flops | bytes accessed | tf_op | source)
XLA Modules:
  0.0 447.7 jit_solution(7515340950392063301)
XLA Ops:
  2.4 11.5 %scatter_custom_fusion = f32[3,128]{0,1:T(8,128)S(1)} fusion(s32[2048]{0:T(1024)S(1)} %copy-done.1, f32[2048,3]{1,0:T(8,128)S(1)} %copy.80, f32[]{:T(128)} %constant.22.clone.1), kind=kCustom, calls=%fused_computation.37 | custom fusion | flops 6144 | bytes 1540 | tf_op jit(solution)/shard_map/vmap()/scatter-add | solution.py:121
  14.0 99.1 %psum.7 = f32[3,128]{0,1:T(8,128)S(1)} all-reduce(f32[3,128]{0,1:T(8,128)S(1)} %scatter_custom_fusion), channel_id=1, replica_groups=mesh['gz'=16,'pa'=32] {'pa'}, use_global_device_ids=true, to_apply=%region_1.0 | all-reduce | flops 384 | bytes 3072 | tf_op jit(solution)/shard_map/psum | solution.py:184
  113.9 114.3 %while.11 = (s32[]{:T(128)}, f32[2,8,3]{1,0,2:T(2,128)S(1)}, f32[2,8,3]{1,0,2:T(2,128)S(1)}, f32[8]{0:T(128)S(1)}, f32[8]{0:T(128)S(1)}, /*index=5*/s32[]{:T(128)}) while((s32[]{:T(128)}, f32[2,8,3]{1,0,2:T(2,128)S(1)}, f32[2,8,3]{1,0,2:T(2,128)S(1)}, f32[8]{0:T(128)S(1)}, f32[8]{0:T(128)S(1)}, /*index=5*/s32[]{:T(128)}) %tuple.64), condition=%wide.region_5.7_spmd.clone, body=%wide.region_4.6_spmd.clone.sunk | while | flops 242 | bytes 1901 | solution.py:172
  113.9 3.4 collective-permute-start
  117.4 4.2 collective-permute-done
  123.5 5.7 %collective-permute-done = f32[2,8,3]{1,0,2:T(2,128)S(1)} collective-permute-done((f32[2,8,3]{1,0,2:T(2,128)S(1)}, f32[2,8,3]{1,0,2:T(2,128)S(1)}, u32[]{:S(2)}, u32[]{:S(2)}) %collective-permute-start) | collective-permute-done | bytes 224 | tf_op jit(solution)/shard_map/while/body/eval_jaxpr/ppermute | solution.py:25
  131.1 5.7 %collective-permute-done = f32[2,8,3]{1,0,2:T(2,128)S(1)} collective-permute-done((f32[2,8,3]{1,0,2:T(2,128)S(1)}, f32[2,8,3]{1,0,2:T(2,128)S(1)}, u32[]{:S(2)}, u32[]{:S(2)}) %collective-permute-start) | collective-permute-done | bytes 224 | tf_op jit(solution)/shard_map/while/body/eval_jaxpr/ppermute | solution.py:25
  138.7 5.7 %collective-permute-done = f32[2,8,3]{1,0,2:T(2,128)S(1)} collective-permute-done((f32[2,8,3]{1,0,2:T(2,128)S(1)}, f32[2,8,3]{1,0,2:T(2,128)S(1)}, u32[]{:S(2)}, u32[]{:S(2)}) %collective-permute-start) | collective-permute-done | bytes 224 | tf_op jit(solution)/shard_map/while/body/eval_jaxpr/ppermute | solution.py:25
  146.4 5.7 %collective-permute-done = f32[2,8,3]{1,0,2:T(2,128)S(1)} collective-permute-done((f32[2,8,3]{1,0,2:T(2,128)S(1)}, f32[2,8,3]{1,0,2:T(2,128)S(1)}, u32[]{:S(2)}, u32[]{:S(2)}) %collective-permute-start) | collective-permute-done | bytes 224 | tf_op jit(solution)/shard_map/while/body/eval_jaxpr/ppermute | solution.py:25
  154.0 5.7 %collective-permute-done = f32[2,8,3]{1,0,2:T(2,128)S(1)} collective-permute-done((f32[2,8,3]{1,0,2:T(2,128)S(1)}, f32[2,8,3]{1,0,2:T(2,128)S(1)}, u32[]{:S(2)}, u32[]{:S(2)}) %collective-permute-start) | collective-permute-done | bytes 224 | tf_op jit(solution)/shard_map/while/body/eval_jaxpr/ppermute | solution.py:25
  161.6 5.7 %collective-permute-done = f32[2,8,3]{1,0,2:T(2,128)S(1)} collective-permute-done((f32[2,8,3]{1,0,2:T(2,128)S(1)}, f32[2,8,3]{1,0,2:T(2,128)S(1)}, u32[]{:S(2)}, u32[]{:S(2)}) %collective-permute-start) | collective-permute-done | bytes 224 | tf_op jit(solution)/shard_map/while/body/eval_jaxpr/ppermute | solution.py:25
  169.2 5.7 %collective-permute-done = f32[2,8,3]{1,0,2:T(2,128)S(1)} collective-permute-done((f32[2,8,3]{1,0,2:T(2,128)S(1)}, f32[2,8,3]{1,0,2:T(2,128)S(1)}, u32[]{:S(2)}, u32[]{:S(2)}) %collective-permute-start) | collective-permute-done | bytes 224 | tf_op jit(solution)/shard_map/while/body/eval_jaxpr/ppermute | solution.py:25
  176.8 5.7 %collective-permute-done = f32[2,8,3]{1,0,2:T(2,128)S(1)} collective-permute-done((f32[2,8,3]{1,0,2:T(2,128)S(1)}, f32[2,8,3]{1,0,2:T(2,128)S(1)}, u32[]{:S(2)}, u32[]{:S(2)}) %collective-permute-start) | collective-permute-done | bytes 224 | tf_op jit(solution)/shard_map/while/body/eval_jaxpr/ppermute | solution.py:25
  184.5 5.7 %collective-permute-done = f32[2,8,3]{1,0,2:T(2,128)S(1)} collective-permute-done((f32[2,8,3]{1,0,2:T(2,128)S(1)}, f32[2,8,3]{1,0,2:T(2,128)S(1)}, u32[]{:S(2)}, u32[]{:S(2)}) %collective-permute-start) | collective-permute-done | bytes 224 | tf_op jit(solution)/shard_map/while/body/eval_jaxpr/ppermute | solution.py:25
  192.1 5.7 %collective-permute-done = f32[2,8,3]{1,0,2:T(2,128)S(1)} collective-permute-done((f32[2,8,3]{1,0,2:T(2,128)S(1)}, f32[2,8,3]{1,0,2:T(2,128)S(1)}, u32[]{:S(2)}, u32[]{:S(2)}) %collective-permute-start) | collective-permute-done | bytes 224 | tf_op jit(solution)/shard_map/while/body/eval_jaxpr/ppermute | solution.py:25
  199.7 5.7 %collective-permute-done = f32[2,8,3]{1,0,2:T(2,128)S(1)} collective-permute-done((f32[2,8,3]{1,0,2:T(2,128)S(1)}, f32[2,8,3]{1,0,2:T(2,128)S(1)}, u32[]{:S(2)}, u32[]{:S(2)}) %collective-permute-start) | collective-permute-done | bytes 224 | tf_op jit(solution)/shard_map/while/body/eval_jaxpr/ppermute | solution.py:25
  207.3 5.7 %collective-permute-done = f32[2,8,3]{1,0,2:T(2,128)S(1)} collective-permute-done((f32[2,8,3]{1,0,2:T(2,128)S(1)}, f32[2,8,3]{1,0,2:T(2,128)S(1)}, u32[]{:S(2)}, u32[]{:S(2)}) %collective-permute-start) | collective-permute-done | bytes 224 | tf_op jit(solution)/shard_map/while/body/eval_jaxpr/ppermute | solution.py:25
  214.9 5.7 %collective-permute-done = f32[2,8,3]{1,0,2:T(2,128)S(1)} collective-permute-done((f32[2,8,3]{1,0,2:T(2,128)S(1)}, f32[2,8,3]{1,0,2:T(2,128)S(1)}, u32[]{:S(2)}, u32[]{:S(2)}) %collective-permute-start) | collective-permute-done | bytes 224 | tf_op jit(solution)/shard_map/while/body/eval_jaxpr/ppermute | solution.py:25
  222.6 5.7 %collective-permute-done = f32[2,8,3]{1,0,2:T(2,128)S(1)} collective-permute-done((f32[2,8,3]{1,0,2:T(2,128)S(1)}, f32[2,8,3]{1,0,2:T(2,128)S(1)}, u32[]{:S(2)}, u32[]{:S(2)}) %collective-permute-start) | collective-permute-done | bytes 224 | tf_op jit(solution)/shard_map/while/body/eval_jaxpr/ppermute | solution.py:25
  228.4 97.2 %gather_fusion.1 = f32[16384]{0:T(1024)S(1)} fusion(f32[128]{0:T(128)S(1)} %get-tuple-element.75, s32[16384]{0:T(1024)S(1)} %bitcast_clamp_fusion), kind=kCustom, calls=%fused_computation.clone | custom fusion | bytes 196608 | tf_op jit(solution)/shard_map/jit(_take)/gather | solution.py:45
  325.8 97.2 %gather_fusion.2 = f32[16384]{0:T(1024)S(1)} fusion(f32[128]{0:T(128)S(1)} %get-tuple-element.76, s32[16384]{0:T(1024)S(1)} %bitcast_clamp_fusion), kind=kCustom, calls=%fused_computation.1.clone | custom fusion | bytes 196608 | tf_op jit(solution)/shard_map/jit(_take)/gather | solution.py:45
  424.3 5.5 %gather_fusion = f32[2048,3]{1,0:T(8,128)S(1)} fusion(f32[3,128]{0,1:T(8,128)S(1)} %copy.82, s32[2048]{0:T(1024)S(1)} %fusion.32), kind=kCustom, calls=%fused_computation.2 | custom fusion | bytes 57344 | tf_op jit(solution)/shard_map/jit(_take)/gather | solution.py:187
  436.3 3.0 collective-permute-done.1
  441.3 5.8 %collective-permute-done.2 = f32[6,384]{1,0:T(8,128)S(1)} collective-permute-done((f32[6,384]{1,0:T(8,128)S(1)}, f32[6,384]{1,0:T(8,128)S(1)}, u32[]{:S(2)}, u32[]{:S(2)}) %collective-permute-start.2) | collective-permute-done | bytes 9248 | tf_op jit(solution)/shard_map/ppermute | solution.py:25
  (101 shorter events, 39.8 us)
Async XLA Ops:
  1.7 0.7 copy-start.1
  13.9 99.1 %copy-start.2 = (f32[4,8]{1,0:T(4,128)S(1)}, f32[4,8]{1,0:T(4,128)}, u32[]{:S(2)}) copy-start(f32[4,8]{1,0:T(4,128)} %param.15) | copy-start | bytes 388
  13.9 99.1 %copy-start.6 = (f32[8]{0:T(128)S(1)}, f32[8]{0:T(128)}, u32[]{:S(2)}) copy-start(f32[8]{0:T(128)} %param.13) | copy-start | bytes 100
  13.9 99.1 %copy-start.7 = (f32[8]{0:T(128)S(1)}, f32[8]{0:T(128)}, u32[]{:S(2)}) copy-start(f32[8]{0:T(128)} %param.14) | copy-start | bytes 100
  113.9 7.6 %collective-permute-start = (f32[2,8,3]{1,0,2:T(2,128)S(1)}, f32[2,8,3]{1,0,2:T(2,128)S(1)}, u32[]{:S(2)}, u32[]{:S(2)}) collective-permute-start(f32[2,8,3]{1,0,2:T(2,128)S(1)} %maximum_add_fusion.2), channel_id=1, source_target_pairs={{0,32},{32,64},{64,96},{96,128},{128,160},{160,192},{192,224},{224... | collective-permute-start | bytes 584 | tf_op jit(solution)/shard_map/while/body/eval_jaxpr/ppermute | solution.py:25
  121.6 7.6 %collective-permute-start = (f32[2,8,3]{1,0,2:T(2,128)S(1)}, f32[2,8,3]{1,0,2:T(2,128)S(1)}, u32[]{:S(2)}, u32[]{:S(2)}) collective-permute-start(f32[2,8,3]{1,0,2:T(2,128)S(1)} %maximum_add_fusion.2), channel_id=1, source_target_pairs={{0,32},{32,64},{64,96},{96,128},{128,160},{160,192},{192,224},{224... | collective-permute-start | bytes 584 | tf_op jit(solution)/shard_map/while/body/eval_jaxpr/ppermute | solution.py:25
  129.2 7.6 %collective-permute-start = (f32[2,8,3]{1,0,2:T(2,128)S(1)}, f32[2,8,3]{1,0,2:T(2,128)S(1)}, u32[]{:S(2)}, u32[]{:S(2)}) collective-permute-start(f32[2,8,3]{1,0,2:T(2,128)S(1)} %maximum_add_fusion.2), channel_id=1, source_target_pairs={{0,32},{32,64},{64,96},{96,128},{128,160},{160,192},{192,224},{224... | collective-permute-start | bytes 584 | tf_op jit(solution)/shard_map/while/body/eval_jaxpr/ppermute | solution.py:25
  136.8 7.6 %collective-permute-start = (f32[2,8,3]{1,0,2:T(2,128)S(1)}, f32[2,8,3]{1,0,2:T(2,128)S(1)}, u32[]{:S(2)}, u32[]{:S(2)}) collective-permute-start(f32[2,8,3]{1,0,2:T(2,128)S(1)} %maximum_add_fusion.2), channel_id=1, source_target_pairs={{0,32},{32,64},{64,96},{96,128},{128,160},{160,192},{192,224},{224... | collective-permute-start | bytes 584 | tf_op jit(solution)/shard_map/while/body/eval_jaxpr/ppermute | solution.py:25
  144.4 7.6 %collective-permute-start = (f32[2,8,3]{1,0,2:T(2,128)S(1)}, f32[2,8,3]{1,0,2:T(2,128)S(1)}, u32[]{:S(2)}, u32[]{:S(2)}) collective-permute-start(f32[2,8,3]{1,0,2:T(2,128)S(1)} %maximum_add_fusion.2), channel_id=1, source_target_pairs={{0,32},{32,64},{64,96},{96,128},{128,160},{160,192},{192,224},{224... | collective-permute-start | bytes 584 | tf_op jit(solution)/shard_map/while/body/eval_jaxpr/ppermute | solution.py:25
  152.0 7.6 %collective-permute-start = (f32[2,8,3]{1,0,2:T(2,128)S(1)}, f32[2,8,3]{1,0,2:T(2,128)S(1)}, u32[]{:S(2)}, u32[]{:S(2)}) collective-permute-start(f32[2,8,3]{1,0,2:T(2,128)S(1)} %maximum_add_fusion.2), channel_id=1, source_target_pairs={{0,32},{32,64},{64,96},{96,128},{128,160},{160,192},{192,224},{224... | collective-permute-start | bytes 584 | tf_op jit(solution)/shard_map/while/body/eval_jaxpr/ppermute | solution.py:25
  159.7 7.6 %collective-permute-start = (f32[2,8,3]{1,0,2:T(2,128)S(1)}, f32[2,8,3]{1,0,2:T(2,128)S(1)}, u32[]{:S(2)}, u32[]{:S(2)}) collective-permute-start(f32[2,8,3]{1,0,2:T(2,128)S(1)} %maximum_add_fusion.2), channel_id=1, source_target_pairs={{0,32},{32,64},{64,96},{96,128},{128,160},{160,192},{192,224},{224... | collective-permute-start | bytes 584 | tf_op jit(solution)/shard_map/while/body/eval_jaxpr/ppermute | solution.py:25
  167.3 7.6 %collective-permute-start = (f32[2,8,3]{1,0,2:T(2,128)S(1)}, f32[2,8,3]{1,0,2:T(2,128)S(1)}, u32[]{:S(2)}, u32[]{:S(2)}) collective-permute-start(f32[2,8,3]{1,0,2:T(2,128)S(1)} %maximum_add_fusion.2), channel_id=1, source_target_pairs={{0,32},{32,64},{64,96},{96,128},{128,160},{160,192},{192,224},{224... | collective-permute-start | bytes 584 | tf_op jit(solution)/shard_map/while/body/eval_jaxpr/ppermute | solution.py:25
  174.9 7.6 %collective-permute-start = (f32[2,8,3]{1,0,2:T(2,128)S(1)}, f32[2,8,3]{1,0,2:T(2,128)S(1)}, u32[]{:S(2)}, u32[]{:S(2)}) collective-permute-start(f32[2,8,3]{1,0,2:T(2,128)S(1)} %maximum_add_fusion.2), channel_id=1, source_target_pairs={{0,32},{32,64},{64,96},{96,128},{128,160},{160,192},{192,224},{224... | collective-permute-start | bytes 584 | tf_op jit(solution)/shard_map/while/body/eval_jaxpr/ppermute | solution.py:25
  182.5 7.6 %collective-permute-start = (f32[2,8,3]{1,0,2:T(2,128)S(1)}, f32[2,8,3]{1,0,2:T(2,128)S(1)}, u32[]{:S(2)}, u32[]{:S(2)}) collective-permute-start(f32[2,8,3]{1,0,2:T(2,128)S(1)} %maximum_add_fusion.2), channel_id=1, source_target_pairs={{0,32},{32,64},{64,96},{96,128},{128,160},{160,192},{192,224},{224... | collective-permute-start | bytes 584 | tf_op jit(solution)/shard_map/while/body/eval_jaxpr/ppermute | solution.py:25
  190.2 7.6 %collective-permute-start = (f32[2,8,3]{1,0,2:T(2,128)S(1)}, f32[2,8,3]{1,0,2:T(2,128)S(1)}, u32[]{:S(2)}, u32[]{:S(2)}) collective-permute-start(f32[2,8,3]{1,0,2:T(2,128)S(1)} %maximum_add_fusion.2), channel_id=1, source_target_pairs={{0,32},{32,64},{64,96},{96,128},{128,160},{160,192},{192,224},{224... | collective-permute-start | bytes 584 | tf_op jit(solution)/shard_map/while/body/eval_jaxpr/ppermute | solution.py:25
  197.8 7.6 %collective-permute-start = (f32[2,8,3]{1,0,2:T(2,128)S(1)}, f32[2,8,3]{1,0,2:T(2,128)S(1)}, u32[]{:S(2)}, u32[]{:S(2)}) collective-permute-start(f32[2,8,3]{1,0,2:T(2,128)S(1)} %maximum_add_fusion.2), channel_id=1, source_target_pairs={{0,32},{32,64},{64,96},{96,128},{128,160},{160,192},{192,224},{224... | collective-permute-start | bytes 584 | tf_op jit(solution)/shard_map/while/body/eval_jaxpr/ppermute | solution.py:25
  205.4 7.6 %collective-permute-start = (f32[2,8,3]{1,0,2:T(2,128)S(1)}, f32[2,8,3]{1,0,2:T(2,128)S(1)}, u32[]{:S(2)}, u32[]{:S(2)}) collective-permute-start(f32[2,8,3]{1,0,2:T(2,128)S(1)} %maximum_add_fusion.2), channel_id=1, source_target_pairs={{0,32},{32,64},{64,96},{96,128},{128,160},{160,192},{192,224},{224... | collective-permute-start | bytes 584 | tf_op jit(solution)/shard_map/while/body/eval_jaxpr/ppermute | solution.py:25
  213.0 7.6 %collective-permute-start = (f32[2,8,3]{1,0,2:T(2,128)S(1)}, f32[2,8,3]{1,0,2:T(2,128)S(1)}, u32[]{:S(2)}, u32[]{:S(2)}) collective-permute-start(f32[2,8,3]{1,0,2:T(2,128)S(1)} %maximum_add_fusion.2), channel_id=1, source_target_pairs={{0,32},{32,64},{64,96},{96,128},{128,160},{160,192},{192,224},{224... | collective-permute-start | bytes 584 | tf_op jit(solution)/shard_map/while/body/eval_jaxpr/ppermute | solution.py:25
  220.6 7.6 %collective-permute-start = (f32[2,8,3]{1,0,2:T(2,128)S(1)}, f32[2,8,3]{1,0,2:T(2,128)S(1)}, u32[]{:S(2)}, u32[]{:S(2)}) collective-permute-start(f32[2,8,3]{1,0,2:T(2,128)S(1)} %maximum_add_fusion.2), channel_id=1, source_target_pairs={{0,32},{32,64},{64,96},{96,128},{128,160},{160,192},{192,224},{224... | collective-permute-start | bytes 584 | tf_op jit(solution)/shard_map/while/body/eval_jaxpr/ppermute | solution.py:25
  430.1 0.9 copy-start
  431.0 0.7 copy-start.4
  433.7 5.6 %collective-permute-start.1 = (f32[6,384]{1,0:T(8,128)S(1)}, f32[6,384]{1,0:T(8,128)S(1)}, u32[]{:S(2)}, u32[]{:S(2)}) collective-permute-start(f32[6,384]{1,0:T(8,128)S(1)} %slice_select_fusion.1), channel_id=1, source_target_pairs={{32,0},{64,32},{96,64},{128,96},{160,128},{192,160},{224,192},{256... | collective-permute-start | bytes 27656 | tf_op jit(solution)/shard_map/ppermute | solution.py:25
  439.4 7.7 %collective-permute-start.2 = (f32[6,384]{1,0:T(8,128)S(1)}, f32[6,384]{1,0:T(8,128)S(1)}, u32[]{:S(2)}, u32[]{:S(2)}) collective-permute-start(f32[6,384]{1,0:T(8,128)S(1)} %get-tuple-element.109), channel_id=1, source_target_pairs={{0,32},{32,64},{64,96},{96,128},{128,160},{160,192},{192,224},{224... | collective-permute-start | bytes 27656 | tf_op jit(solution)/shard_map/ppermute | solution.py:25
  447.1 0.6 copy-start.5
  (1 other events, 0.6 us)
where the time goes:
time: 450 us; the launch traced here: 448 us
  local copies, waits for them, and re-layouts  204 us (45%)
  blocking collectives  99.1 us (22%)
  waiting for transfers between devices  92.3 us (21%)
  starting transfers between devices  34.1 us (8%)
  other arithmetic  15 us (3%)
    gather x2, local copies, waits for them, and re-layouts, toeplitz(): picked = jnp.take(wave, jnp.clip(offset, 0, slab_width - 1))  194 us
    psum x1, blocking collectives, body(): moments = lax.psum(partial_moments, 'pa')  99.1 us
    ppermute x17, waiting for transfers between devices, from_behind_2(): lax.ppermute(value, axis, [(source, source + steps) for source in range(l...  92.3 us
    ppermute x17, starting transfers between devices, from_behind_2(): lax.ppermute(value, axis, [(source, source + steps) for source in range(l...  34.1 us
    scatter-add x1, other arithmetic, deposit(): jax.ops.segment_sum(column, index, num_segments=segments)  11.5 us
  transfers between devices with their start and end apart: 17, of which 17 were waited for; matrix products, arithmetic and copies ran while one was open for 0% of the time, Pallas kernels for 0%

commit v1 on v0

--- a/solution.py
+++ b/solution.py
@@ -17,6 +17,18 @@
 voltage = 0.05
 synch_phase = 0.3
 slippage = 0.1
+
+
+def settle_files(x0, ax_name):
+    shares = lax.axis_size(ax_name)
+    block_out, big = (x0, 0)
+    while 1 << big < shares:
+        moved = lax.ppermute(
+            block_out, ax_name, [(dev_i, dev_i ^ 1 << big) for dev_i in range(shares)]
+        )
+        block_out = block_out + moved
+        big = big + 1
+    return block_out
 
 
 def from_behind_2(value, axis, steps):
@@ -181,7 +193,7 @@
     mean_fill = local_count * member_count / slab_width
     values = moment_values(particles, mean_fill)
     partial_moments = deposit(values, slice_index, slab_width)
-    moments = lax.psum(partial_moments, "pa")
+    moments = settle_files(partial_moments, "pa")
     carried = upstream(slab_summary(moments, tables), tables[6], slab_count)
     wake_kick = slab_kick(moments, carried, tables)
     per_particle = jnp.take(wake_kick, slice_index, axis=1)

time: 450 us -> 396 us (0.88)
  blocking collectives: 99.1 us -> 0 us
  starting transfers between devices: 34.1 us -> 66.7 us
  waiting for transfers between devices: 92.3 us -> 104 us
    psum x1 -> x0, blocking collectives: 99.1 us -> none  [body(): moments = lax.psum(partial_moments, 'pa')]
    ppermute x0 -> x5, starting transfers between devices: none -> 32.6 us  [settle_files(): lax.ppermute(block_out, ax_name, [(dev_i, dev_i ^ 1 << big) for dev_i in...]
    ppermute x0 -> x5, waiting for transfers between devices: none -> 10.9 us  [settle_files(): lax.ppermute(block_out, ax_name, [(dev_i, dev_i ^ 1 << big) for dev_i in...]
  transfers between devices with their start and end apart: 17 -> 22, of which waited for: 17 -> 20; matrix products, arithmetic and copies ran while one was open for 0% -> 50% of each run, Pallas kernels for 0% -> 0%
where the time goes in v1:
time: 396 us; the launch traced here: 394 us
  local copies, waits for them, and re-layouts  205 us (52%)
  waiting for transfers between devices  104 us (26%)
  starting transfers between devices  66.7 us (17%)
  other arithmetic  15 us (4%)
    gather x2, local copies, waits for them, and re-layouts, toeplitz(): picked = jnp.take(wave, jnp.clip(offset, 0, slab_width - 1))  194 us
    ppermute x17, waiting for transfers between devices, from_behind_2(): lax.ppermute(value, axis, [(source, source + steps) for source in range(l...  92.9 us
    ppermute x17, starting transfers between devices, from_behind_2(): lax.ppermute(value, axis, [(source, source + steps) for source in range(l...  34.1 us
    ppermute x5, starting transfers between devices, settle_files(): lax.ppermute(block_out, ax_name, [(dev_i, dev_i ^ 1 << big) for dev_i in...  32.6 us
    scatter-add x1, other arithmetic, deposit(): jax.ops.segment_sum(column, index, num_segments=segments)  11.5 us
    ppermute x5, waiting for transfers between devices, settle_files(): lax.ppermute(block_out, ax_name, [(dev_i, dev_i ^ 1 << big) for dev_i in...  10.9 us
  transfers between devices with their start and end apart: 22, of which 20 were waited for; matrix products, arithmetic and copies ran while one was open for 50% of the time, Pallas kernels for 0%

profile of v1, /device:TPU:16, one launch (start us, length us, event | category | flops | bytes accessed | tf_op | source)
XLA Modules:
  0.0 394.0 jit_solution(1549594771581674540)
XLA Ops:
  2.4 11.5 %scatter_custom_fusion = f32[3,128]{0,1:T(8,128)S(1)} fusion(s32[2048]{0:T(1024)S(1)} %copy-done.1, f32[2048,3]{1,0:T(8,128)S(1)} %copy.80, f32[]{:T(128)} %constant.22.clone.1), kind=kCustom, calls=%fused_computation.36 | custom fusion | flops 6144 | bytes 1540 | tf_op jit(solution)/shard_map/vmap()/scatter-add | solution.py:133
  23.9 5.2 %collective-permute-start.3 = (f32[3,128]{0,1:T(8,128)S(1)}, f32[3,128]{0,1:T(8,128)S(1)}, u32[]{:S(2)}, u32[]{:S(2)}) collective-permute-start(f32[3,128]{0,1:T(8,128)S(1)} %add.153), channel_id=1, source_target_pairs={{0,4},{1,5},{2,6},{3,7},{4,0},{5,1},{6,2},{7,3},{8,12},{9,13},{10,... | collective-permute-start | bytes 4616 | tf_op jit(solution)/shard_map/ppermute | solution.py:26
  32.8 9.1 %collective-permute-start.4 = (f32[3,128]{0,1:T(8,128)S(1)}, f32[3,128]{0,1:T(8,128)S(1)}, u32[]{:S(2)}, u32[]{:S(2)}) collective-permute-start(f32[3,128]{0,1:T(8,128)S(1)} %add.154), channel_id=1, source_target_pairs={{0,8},{1,9},{2,10},{3,11},{4,12},{5,13},{6,14},{7,15},{8,0},{9,1},... | collective-permute-start | bytes 4616 | tf_op jit(solution)/shard_map/ppermute | solution.py:26
  41.9 5.2 %collective-permute-done.4 = f32[3,128]{0,1:T(8,128)S(1)} collective-permute-done((f32[3,128]{0,1:T(8,128)S(1)}, f32[3,128]{0,1:T(8,128)S(1)}, u32[]{:S(2)}, u32[]{:S(2)}) %collective-permute-start.4) | collective-permute-done | bytes 1568 | tf_op jit(solution)/shard_map/ppermute | solution.py:26
  47.1 12.6 %collective-permute-start.5 = (f32[3,128]{0,1:T(8,128)S(1)}, f32[3,128]{0,1:T(8,128)S(1)}, u32[]{:S(2)}, u32[]{:S(2)}) collective-permute-start(f32[3,128]{0,1:T(8,128)S(1)} %add.155), channel_id=1, source_target_pairs={{0,16},{1,17},{2,18},{3,19},{4,20},{5,21},{6,22},{7,23},{8,24},{9,... | collective-permute-start | bytes 4616 | tf_op jit(solution)/shard_map/ppermute | solution.py:26
  60.3 97.2 %gather_fusion.1 = f32[16384]{0:T(1024)S(1)} fusion(f32[128]{0:T(128)S(1)} %get-tuple-element.75, s32[16384]{0:T(1024)S(1)} %bitcast_clamp_fusion), kind=kCustom, calls=%fused_computation.clone | custom fusion | bytes 196608 | tf_op jit(solution)/shard_map/jit(_take)/gather | solution.py:57
  157.6 97.2 %gather_fusion.2 = f32[16384]{0:T(1024)S(1)} fusion(f32[128]{0:T(128)S(1)} %get-tuple-element.76, s32[16384]{0:T(1024)S(1)} %bitcast_clamp_fusion), kind=kCustom, calls=%fused_computation.1.clone | custom fusion | bytes 196608 | tf_op jit(solution)/shard_map/jit(_take)/gather | solution.py:57
  256.2 114.3 %while.11 = (s32[]{:T(128)}, f32[2,8,3]{1,0,2:T(2,128)S(1)}, f32[2,8,3]{1,0,2:T(2,128)S(1)}, f32[8]{0:T(128)S(1)}, f32[8]{0:T(128)S(1)}, /*index=5*/s32[]{:T(128)}) while((s32[]{:T(128)}, f32[2,8,3]{1,0,2:T(2,128)S(1)}, f32[2,8,3]{1,0,2:T(2,128)S(1)}, f32[8]{0:T(128)S(1)}, f32[8]{0:T(128)S(1)}, /*index=5*/s32[]{:T(128)}) %tuple.64), condition=%wide.region_4.6_spmd.clone, body=%wide.region_3.5_spmd.clone.sunk | while | flops 242 | bytes 1901 | solution.py:184
  265.8 5.7 %collective-permute-done = f32[2,8,3]{1,0,2:T(2,128)S(1)} collective-permute-done((f32[2,8,3]{1,0,2:T(2,128)S(1)}, f32[2,8,3]{1,0,2:T(2,128)S(1)}, u32[]{:S(2)}, u32[]{:S(2)}) %collective-permute-start) | collective-permute-done | bytes 224 | tf_op jit(solution)/shard_map/while/body/eval_jaxpr/ppermute | solution.py:37
  273.4 5.7 %collective-permute-done = f32[2,8,3]{1,0,2:T(2,128)S(1)} collective-permute-done((f32[2,8,3]{1,0,2:T(2,128)S(1)}, f32[2,8,3]{1,0,2:T(2,128)S(1)}, u32[]{:S(2)}, u32[]{:S(2)}) %collective-permute-start) | collective-permute-done | bytes 224 | tf_op jit(solution)/shard_map/while/body/eval_jaxpr/ppermute | solution.py:37
  281.0 5.7 %collective-permute-done = f32[2,8,3]{1,0,2:T(2,128)S(1)} collective-permute-done((f32[2,8,3]{1,0,2:T(2,128)S(1)}, f32[2,8,3]{1,0,2:T(2,128)S(1)}, u32[]{:S(2)}, u32[]{:S(2)}) %collective-permute-start) | collective-permute-done | bytes 224 | tf_op jit(solution)/shard_map/while/body/eval_jaxpr/ppermute | solution.py:37
  288.7 5.7 %collective-permute-done = f32[2,8,3]{1,0,2:T(2,128)S(1)} collective-permute-done((f32[2,8,3]{1,0,2:T(2,128)S(1)}, f32[2,8,3]{1,0,2:T(2,128)S(1)}, u32[]{:S(2)}, u32[]{:S(2)}) %collective-permute-start) | collective-permute-done | bytes 224 | tf_op jit(solution)/shard_map/while/body/eval_jaxpr/ppermute | solution.py:37
  296.3 5.7 %collective-permute-done = f32[2,8,3]{1,0,2:T(2,128)S(1)} collective-permute-done((f32[2,8,3]{1,0,2:T(2,128)S(1)}, f32[2,8,3]{1,0,2:T(2,128)S(1)}, u32[]{:S(2)}, u32[]{:S(2)}) %collective-permute-start) | collective-permute-done | bytes 224 | tf_op jit(solution)/shard_map/while/body/eval_jaxpr/ppermute | solution.py:37
  303.9 5.7 %collective-permute-done = f32[2,8,3]{1,0,2:T(2,128)S(1)} collective-permute-done((f32[2,8,3]{1,0,2:T(2,128)S(1)}, f32[2,8,3]{1,0,2:T(2,128)S(1)}, u32[]{:S(2)}, u32[]{:S(2)}) %collective-permute-start) | collective-permute-done | bytes 224 | tf_op jit(solution)/shard_map/while/body/eval_jaxpr/ppermute | solution.py:37
  311.5 5.7 %collective-permute-done = f32[2,8,3]{1,0,2:T(2,128)S(1)} collective-permute-done((f32[2,8,3]{1,0,2:T(2,128)S(1)}, f32[2,8,3]{1,0,2:T(2,128)S(1)}, u32[]{:S(2)}, u32[]{:S(2)}) %collective-permute-start) | collective-permute-done | bytes 224 | tf_op jit(solution)/shard_map/while/body/eval_jaxpr/ppermute | solution.py:37
  319.1 5.7 %collective-permute-done = f32[2,8,3]{1,0,2:T(2,128)S(1)} collective-permute-done((f32[2,8,3]{1,0,2:T(2,128)S(1)}, f32[2,8,3]{1,0,2:T(2,128)S(1)}, u32[]{:S(2)}, u32[]{:S(2)}) %collective-permute-start) | collective-permute-done | bytes 224 | tf_op jit(solution)/shard_map/while/body/eval_jaxpr/ppermute | solution.py:37
  326.8 5.7 %collective-permute-done = f32[2,8,3]{1,0,2:T(2,128)S(1)} collective-permute-done((f32[2,8,3]{1,0,2:T(2,128)S(1)}, f32[2,8,3]{1,0,2:T(2,128)S(1)}, u32[]{:S(2)}, u32[]{:S(2)}) %collective-permute-start) | collective-permute-done | bytes 224 | tf_op jit(solution)/shard_map/while/body/eval_jaxpr/ppermute | solution.py:37
  334.4 5.7 %collective-permute-done = f32[2,8,3]{1,0,2:T(2,128)S(1)} collective-permute-done((f32[2,8,3]{1,0,2:T(2,128)S(1)}, f32[2,8,3]{1,0,2:T(2,128)S(1)}, u32[]{:S(2)}, u32[]{:S(2)}) %collective-permute-start) | collective-permute-done | bytes 224 | tf_op jit(solution)/shard_map/while/body/eval_jaxpr/ppermute | solution.py:37
  342.0 5.7 %collective-permute-done = f32[2,8,3]{1,0,2:T(2,128)S(1)} collective-permute-done((f32[2,8,3]{1,0,2:T(2,128)S(1)}, f32[2,8,3]{1,0,2:T(2,128)S(1)}, u32[]{:S(2)}, u32[]{:S(2)}) %collective-permute-start) | collective-permute-done | bytes 224 | tf_op jit(solution)/shard_map/while/body/eval_jaxpr/ppermute | solution.py:37
  349.6 5.7 %collective-permute-done = f32[2,8,3]{1,0,2:T(2,128)S(1)} collective-permute-done((f32[2,8,3]{1,0,2:T(2,128)S(1)}, f32[2,8,3]{1,0,2:T(2,128)S(1)}, u32[]{:S(2)}, u32[]{:S(2)}) %collective-permute-start) | collective-permute-done | bytes 224 | tf_op jit(solution)/shard_map/while/body/eval_jaxpr/ppermute | solution.py:37
  357.2 5.7 %collective-permute-done = f32[2,8,3]{1,0,2:T(2,128)S(1)} collective-permute-done((f32[2,8,3]{1,0,2:T(2,128)S(1)}, f32[2,8,3]{1,0,2:T(2,128)S(1)}, u32[]{:S(2)}, u32[]{:S(2)}) %collective-permute-start) | collective-permute-done | bytes 224 | tf_op jit(solution)/shard_map/while/body/eval_jaxpr/ppermute | solution.py:37
  364.9 5.7 %collective-permute-done = f32[2,8,3]{1,0,2:T(2,128)S(1)} collective-permute-done((f32[2,8,3]{1,0,2:T(2,128)S(1)}, f32[2,8,3]{1,0,2:T(2,128)S(1)}, u32[]{:S(2)}, u32[]{:S(2)}) %collective-permute-start) | collective-permute-done | bytes 224 | tf_op jit(solution)/shard_map/while/body/eval_jaxpr/ppermute | solution.py:37
  372.1 5.5 %gather_fusion = f32[2048,3]{1,0:T(8,128)S(1)} fusion(f32[3,128]{0,1:T(8,128)S(1)} %copy.82, s32[2048]{0:T(1024)S(1)} %fusion.31), kind=kCustom, calls=%fused_computation.2 | custom fusion | bytes 57344 | tf_op jit(solution)/shard_map/jit(_take)/gather | solution.py:199
  387.6 5.8 %collective-permute-done.7 = f32[6,384]{1,0:T(8,128)S(1)} collective-permute-done((f32[6,384]{1,0:T(8,128)S(1)}, f32[6,384]{1,0:T(8,128)S(1)}, u32[]{:S(2)}, u32[]{:S(2)}) %collective-permute-start.7) | collective-permute-done | bytes 9248 | tf_op jit(solution)/shard_map/ppermute | solution.py:37
  (115 shorter events, 63.7 us)
Async XLA Ops:
  13.9 3.4 collective-permute-start.1
  17.3 6.6 %collective-permute-start.2 = (f32[3,128]{0,1:T(8,128)S(1)}, f32[3,128]{0,1:T(8,128)S(1)}, u32[]{:S(2)}, u32[]{:S(2)}) collective-permute-start(f32[3,128]{0,1:T(8,128)S(1)} %add.152), channel_id=1, source_target_pairs={{0,2},{1,3},{2,0},{3,1},{4,6},{5,7},{6,4},{7,5},{8,10},{9,11},{10,... | collective-permute-start | bytes 4616 | tf_op jit(solution)/shard_map/ppermute | solution.py:26
  21.3 7.8 %copy-start.4 = (s32[1,1,2]{2,1,0:T(1,128)S(1)}, s32[1,1,2]{2,1,0:T(1,128)}, u32[]{:S(2)}) copy-start(s32[1,1,2]{2,1,0:T(1,128)} %param.12) | copy-start | bytes 28
  23.9 8.8 %collective-permute-start.3 = (f32[3,128]{0,1:T(8,128)S(1)}, f32[3,128]{0,1:T(8,128)S(1)}, u32[]{:S(2)}, u32[]{:S(2)}) collective-permute-start(f32[3,128]{0,1:T(8,128)S(1)} %add.153), channel_id=1, source_target_pairs={{0,4},{1,5},{2,6},{3,7},{4,0},{5,1},{6,2},{7,3},{8,12},{9,13},{10,... | collective-permute-start | bytes 4616 | tf_op jit(solution)/shard_map/ppermute | solution.py:26
  32.8 14.3 %collective-permute-start.4 = (f32[3,128]{0,1:T(8,128)S(1)}, f32[3,128]{0,1:T(8,128)S(1)}, u32[]{:S(2)}, u32[]{:S(2)}) collective-permute-start(f32[3,128]{0,1:T(8,128)S(1)} %add.154), channel_id=1, source_target_pairs={{0,8},{1,9},{2,10},{3,11},{4,12},{5,13},{6,14},{7,15},{8,0},{9,1},... | collective-permute-start | bytes 4616 | tf_op jit(solution)/shard_map/ppermute | solution.py:26
  47.1 208.3 %collective-permute-start.5 = (f32[3,128]{0,1:T(8,128)S(1)}, f32[3,128]{0,1:T(8,128)S(1)}, u32[]{:S(2)}, u32[]{:S(2)}) collective-permute-start(f32[3,128]{0,1:T(8,128)S(1)} %add.155), channel_id=1, source_target_pairs={{0,16},{1,17},{2,18},{3,19},{4,20},{5,21},{6,22},{7,23},{8,24},{9,... | collective-permute-start | bytes 4616 | tf_op jit(solution)/shard_map/ppermute | solution.py:26
  256.3 7.6 %collective-permute-start = (f32[2,8,3]{1,0,2:T(2,128)S(1)}, f32[2,8,3]{1,0,2:T(2,128)S(1)}, u32[]{:S(2)}, u32[]{:S(2)}) collective-permute-start(f32[2,8,3]{1,0,2:T(2,128)S(1)} %maximum_add_fusion.3), channel_id=1, source_target_pairs={{0,32},{32,64},{64,96},{96,128},{128,160},{160,192},{192,224},{224... | collective-permute-start | bytes 584 | tf_op jit(solution)/shard_map/while/body/eval_jaxpr/ppermute | solution.py:37
  263.9 7.6 %collective-permute-start = (f32[2,8,3]{1,0,2:T(2,128)S(1)}, f32[2,8,3]{1,0,2:T(2,128)S(1)}, u32[]{:S(2)}, u32[]{:S(2)}) collective-permute-start(f32[2,8,3]{1,0,2:T(2,128)S(1)} %maximum_add_fusion.3), channel_id=1, source_target_pairs={{0,32},{32,64},{64,96},{96,128},{128,160},{160,192},{192,224},{224... | collective-permute-start | bytes 584 | tf_op jit(solution)/shard_map/while/body/eval_jaxpr/ppermute | solution.py:37
  271.5 7.6 %collective-permute-start = (f32[2,8,3]{1,0,2:T(2,128)S(1)}, f32[2,8,3]{1,0,2:T(2,128)S(1)}, u32[]{:S(2)}, u32[]{:S(2)}) collective-permute-start(f32[2,8,3]{1,0,2:T(2,128)S(1)} %maximum_add_fusion.3), channel_id=1, source_target_pairs={{0,32},{32,64},{64,96},{96,128},{128,160},{160,192},{192,224},{224... | collective-permute-start | bytes 584 | tf_op jit(solution)/shard_map/while/body/eval_jaxpr/ppermute | solution.py:37
  279.1 7.6 %collective-permute-start = (f32[2,8,3]{1,0,2:T(2,128)S(1)}, f32[2,8,3]{1,0,2:T(2,128)S(1)}, u32[]{:S(2)}, u32[]{:S(2)}) collective-permute-start(f32[2,8,3]{1,0,2:T(2,128)S(1)} %maximum_add_fusion.3), channel_id=1, source_target_pairs={{0,32},{32,64},{64,96},{96,128},{128,160},{160,192},{192,224},{224... | collective-permute-start | bytes 584 | tf_op jit(solution)/shard_map/while/body/eval_jaxpr/ppermute | solution.py:37
  286.7 7.6 %collective-permute-start = (f32[2,8,3]{1,0,2:T(2,128)S(1)}, f32[2,8,3]{1,0,2:T(2,128)S(1)}, u32[]{:S(2)}, u32[]{:S(2)}) collective-permute-start(f32[2,8,3]{1,0,2:T(2,128)S(1)} %maximum_add_fusion.3), channel_id=1, source_target_pairs={{0,32},{32,64},{64,96},{96,128},{128,160},{160,192},{192,224},{224... | collective-permute-start | bytes 584 | tf_op jit(solution)/shard_map/while/body/eval_jaxpr/ppermute | solution.py:37
  294.4 7.6 %collective-permute-start = (f32[2,8,3]{1,0,2:T(2,128)S(1)}, f32[2,8,3]{1,0,2:T(2,128)S(1)}, u32[]{:S(2)}, u32[]{:S(2)}) collective-permute-start(f32[2,8,3]{1,0,2:T(2,128)S(1)} %maximum_add_fusion.3), channel_id=1, source_target_pairs={{0,32},{32,64},{64,96},{96,128},{128,160},{160,192},{192,224},{224... | collective-permute-start | bytes 584 | tf_op jit(solution)/shard_map/while/body/eval_jaxpr/ppermute | solution.py:37
  302.0 7.6 %collective-permute-start = (f32[2,8,3]{1,0,2:T(2,128)S(1)}, f32[2,8,3]{1,0,2:T(2,128)S(1)}, u32[]{:S(2)}, u32[]{:S(2)}) collective-permute-start(f32[2,8,3]{1,0,2:T(2,128)S(1)} %maximum_add_fusion.3), channel_id=1, source_target_pairs={{0,32},{32,64},{64,96},{96,128},{128,160},{160,192},{192,224},{224... | collective-permute-start | bytes 584 | tf_op jit(solution)/shard_map/while/body/eval_jaxpr/ppermute | solution.py:37
  309.6 7.6 %collective-permute-start = (f32[2,8,3]{1,0,2:T(2,128)S(1)}, f32[2,8,3]{1,0,2:T(2,128)S(1)}, u32[]{:S(2)}, u32[]{:S(2)}) collective-permute-start(f32[2,8,3]{1,0,2:T(2,128)S(1)} %maximum_add_fusion.3), channel_id=1, source_target_pairs={{0,32},{32,64},{64,96},{96,128},{128,160},{160,192},{192,224},{224... | collective-permute-start | bytes 584 | tf_op jit(solution)/shard_map/while/body/eval_jaxpr/ppermute | solution.py:37
  317.2 7.6 %collective-permute-start = (f32[2,8,3]{1,0,2:T(2,128)S(1)}, f32[2,8,3]{1,0,2:T(2,128)S(1)}, u32[]{:S(2)}, u32[]{:S(2)}) collective-permute-start(f32[2,8,3]{1,0,2:T(2,128)S(1)} %maximum_add_fusion.3), channel_id=1, source_target_pairs={{0,32},{32,64},{64,96},{96,128},{128,160},{160,192},{192,224},{224... | collective-permute-start | bytes 584 | tf_op jit(solution)/shard_map/while/body/eval_jaxpr/ppermute | solution.py:37
  324.8 7.6 %collective-permute-start = (f32[2,8,3]{1,0,2:T(2,128)S(1)}, f32[2,8,3]{1,0,2:T(2,128)S(1)}, u32[]{:S(2)}, u32[]{:S(2)}) collective-permute-start(f32[2,8,3]{1,0,2:T(2,128)S(1)} %maximum_add_fusion.3), channel_id=1, source_target_pairs={{0,32},{32,64},{64,96},{96,128},{128,160},{160,192},{192,224},{224... | collective-permute-start | bytes 584 | tf_op jit(solution)/shard_map/while/body/eval_jaxpr/ppermute | solution.py:37
  332.5 7.6 %collective-permute-start = (f32[2,8,3]{1,0,2:T(2,128)S(1)}, f32[2,8,3]{1,0,2:T(2,128)S(1)}, u32[]{:S(2)}, u32[]{:S(2)}) collective-permute-start(f32[2,8,3]{1,0,2:T(2,128)S(1)} %maximum_add_fusion.3), channel_id=1, source_target_pairs={{0,32},{32,64},{64,96},{96,128},{128,160},{160,192},{192,224},{224... | collective-permute-start | bytes 584 | tf_op jit(solution)/shard_map/while/body/eval_jaxpr/ppermute | solution.py:37
  340.1 7.6 %collective-permute-start = (f32[2,8,3]{1,0,2:T(2,128)S(1)}, f32[2,8,3]{1,0,2:T(2,128)S(1)}, u32[]{:S(2)}, u32[]{:S(2)}) collective-permute-start(f32[2,8,3]{1,0,2:T(2,128)S(1)} %maximum_add_fusion.3), channel_id=1, source_target_pairs={{0,32},{32,64},{64,96},{96,128},{128,160},{160,192},{192,224},{224... | collective-permute-start | bytes 584 | tf_op jit(solution)/shard_map/while/body/eval_jaxpr/ppermute | solution.py:37
  347.7 7.6 %collective-permute-start = (f32[2,8,3]{1,0,2:T(2,128)S(1)}, f32[2,8,3]{1,0,2:T(2,128)S(1)}, u32[]{:S(2)}, u32[]{:S(2)}) collective-permute-start(f32[2,8,3]{1,0,2:T(2,128)S(1)} %maximum_add_fusion.3), channel_id=1, source_target_pairs={{0,32},{32,64},{64,96},{96,128},{128,160},{160,192},{192,224},{224... | collective-permute-start | bytes 584 | tf_op jit(solution)/shard_map/while/body/eval_jaxpr/ppermute | solution.py:37
  355.3 7.6 %collective-permute-start = (f32[2,8,3]{1,0,2:T(2,128)S(1)}, f32[2,8,3]{1,0,2:T(2,128)S(1)}, u32[]{:S(2)}, u32[]{:S(2)}) collective-permute-start(f32[2,8,3]{1,0,2:T(2,128)S(1)} %maximum_add_fusion.3), channel_id=1, source_target_pairs={{0,32},{32,64},{64,96},{96,128},{128,160},{160,192},{192,224},{224... | collective-permute-start | bytes 584 | tf_op jit(solution)/shard_map/while/body/eval_jaxpr/ppermute | solution.py:37
  362.9 7.6 %collective-permute-start = (f32[2,8,3]{1,0,2:T(2,128)S(1)}, f32[2,8,3]{1,0,2:T(2,128)S(1)}, u32[]{:S(2)}, u32[]{:S(2)}) collective-permute-start(f32[2,8,3]{1,0,2:T(2,128)S(1)} %maximum_add_fusion.3), channel_id=1, source_target_pairs={{0,32},{32,64},{64,96},{96,128},{128,160},{160,192},{192,224},{224... | collective-permute-start | bytes 584 | tf_op jit(solution)/shard_map/while/body/eval_jaxpr/ppermute | solution.py:37
  377.9 0.9 copy-start
  380.1 5.6 %collective-permute-start.6 = (f32[6,384]{1,0:T(8,128)S(1)}, f32[6,384]{1,0:T(8,128)S(1)}, u32[]{:S(2)}, u32[]{:S(2)}) collective-permute-start(f32[6,384]{1,0:T(8,128)S(1)} %slice_select_fusion.1), channel_id=1, source_target_pairs={{32,0},{64,32},{96,64},{128,96},{160,128},{192,160},{224,192},{256... | collective-permute-start | bytes 27656 | tf_op jit(solution)/shard_map/ppermute | solution.py:37
  385.7 7.7 %collective-permute-start.7 = (f32[6,384]{1,0:T(8,128)S(1)}, f32[6,384]{1,0:T(8,128)S(1)}, u32[]{:S(2)}, u32[]{:S(2)}) collective-permute-start(f32[6,384]{1,0:T(8,128)S(1)} %get-tuple-element.109), channel_id=1, source_target_pairs={{0,32},{32,64},{64,96},{96,128},{128,160},{160,192},{192,224},{224... | collective-permute-start | bytes 27656 | tf_op jit(solution)/shard_map/ppermute | solution.py:37
  (6 other events, 3.9 us)
